TPU v7x, 32 devices: a whole 2x2x4 slice. The times are simulated.
32 devices in a mesh: groups: 2 (over x), tm: 16 (over z, y, core).
Axes of the slice: x: 2, y: 2, z: 4, core: 2. Of those that a mesh axis runs over, the one named last changes fastest.
Arguments:
- records: bfloat16 [384, 4096], P('groups', 'tm'), parts along dimension 0, may hold values from -6 to 6
- bank: bfloat16 [256, 384, 240], P('tm', 'groups'), parts along dimension 1, may hold values from -6 to 6
- plan: int32 [6], P('groups'), parts along dimension 0, may hold values from 0 to 15
- template_ids: int32 [6, 2], P('groups'), parts along dimension 0, may hold values from 0 to 15
- channel_mask: int32 [384], P('groups'), parts along dimension 0, may hold values 0 or 1
Outputs:
- detection: float32 [6, 2, 4096], P('groups', None, 'tm'), parts along dimension 0
There are 2 independent parts, one for each index of `groups`. A program takes and returns all parts, laid end to end along the dimension named above; each array names one. Nothing has to cross between parts.
Inputs may be any that keep to these rules, and one draw needn't show every extreme that they name: `plan`: the index of tm that holds a step's templates. `template_ids`: slots within the owner's 16 templates.
All inputs are finite; a program needn't handle non-finite values.
Results may differ from a plain program's by a relative error of at most 0.0003.
Values may be sent and summed in bfloat16 or wider, within the bound.
A program may use at most 64 MiB of HBM per device.

v0:
```python
import jax
import jax.numpy as jnp
from jax import lax
from jax.sharding import PartitionSpec as P


def passed_along(block, axis, distance):
    devices = range(lax.axis_size(axis))
    route = [(i - distance, i) for i in devices if i - distance in devices]
    return lax.ppermute(block, axis, route)


def correlate(extended, chosen, inv_norm, mask_f, scale):
    kcount, chans, taps = chosen.shape
    kernel = jnp.transpose(chosen, (1, 0, 2)).reshape(chans * kcount, 1, taps)
    raw = lax.conv_general_dilated(
        extended[None],
        kernel,
        (1,),
        "VALID",
        dimension_numbers=("NCH", "OIH", "NCH"),
        feature_group_count=chans,
        preferred_element_type=jnp.float32,
    )[0]
    raw = raw.reshape(chans, kcount, -1)
    chosen_f = chosen.astype(jnp.float32)
    weight = mask_f[None, :] / jnp.sqrt(jnp.sum(chosen_f * chosen_f, axis=2) + 1e-06)
    normed = raw * inv_norm[:, None, :]
    return scale * jnp.einsum("kc,ckt->kt", weight, normed, precision=lax.Precision.HIGHEST)


def shards(records, bank, plan, template_ids, channel_mask):
    taps = bank.shape[2]
    slots = bank.shape[0]
    steps = plan.shape[0]
    tail = passed_along(records[:, : taps - 1], "tm", -1)
    extended = jnp.concatenate([records, tail], axis=1)
    sq = extended.astype(jnp.float32) ** 2
    energy = lax.reduce_window(sq, jnp.array(0.0, sq.dtype), lax.add, (1, taps), (1, 1), "VALID")
    inv_norm = 1.0 / jnp.sqrt(energy + 1e-06)
    mask_f = channel_mask.astype(jnp.float32)
    scale = jnp.sqrt(taps / (1.0 + jnp.sum(mask_f)))
    onehot = (template_ids[:, :, None] == jnp.arange(slots, dtype=jnp.int32)[None, None, :]).astype(
        jnp.bfloat16
    )
    picked = jnp.einsum("skb,bcl->skcl", onehot, bank, preferred_element_type=jnp.float32).astype(
        jnp.bfloat16
    )
    results = []
    owned = plan == lax.axis_index("tm")
    contrib = jnp.where(owned[:, None, None, None], picked.astype(jnp.float32), 0.0)
    gathered = lax.psum(contrib, "tm").astype(jnp.bfloat16)
    for step in range(steps):
        results.append(correlate(extended, gathered[step], inv_norm, mask_f, scale))
    return jnp.stack(results, axis=0)


def solution(mesh):
    placed = (
        P("groups", "tm"),
        P("tm", "groups", None),
        P("groups"),
        P("groups", None),
        P("groups"),
    )
    return jax.shard_map(
        shards, mesh=mesh, in_specs=placed, out_specs=P("groups", None, "tm"), check_vma=False
    )
```

profile of v0, /device:TPU:0, one launch (start us, length us, event | category | flops | bytes accessed | tf_op | source)
XLA Modules:
  0.0 188.6 jit_solution(4529807161616431503)
XLA Ops:
  0.0 1.3 collective-permute-start
  1.3 0.7 broadcast_compare_fusion
  2.0 2.5 %convert_select_fusion = f32[3,2,192,240]{3,0,2,1:T(4,128)S(1)} fusion(bf16[16,192,240]{2,1,0:T(8,128)(2,1)} %param.6, pred[3]{0:T(512)(128)(4,1)S(1)} %broadcast_compare_fusion, s32[3,2]{0,1:T(2,128)} %param.8), kind=kOutput, calls=%fused_computation.3 | convolution fusion | flops 9676896 | bytes 2580507 | tf_op jit(solution)/shard_map/skb,bcl->skcl/dot_general | solution.py:46
  4.5 77.2 %all-reduce.1 = bf16[3,2,192,240]{3,0,2,1:T(4,128)(2,1)S(1)} all-reduce(f32[3,2,192,240]{3,0,2,1:T(4,128)S(1)} %convert_select_fusion), channel_id=1, replica_groups=mesh['groups'=2,'tm'=16] {'tm'}, use_global_device_ids=true, to_apply=%region_1.0 | all-reduce | flops 276480 | bytes 1658880 | tf_op jit(solution)/shard_map/psum | solution.py:52
  81.7 0.8 fusion.23
  82.6 0.2 multiply_reduce_fusion
  82.9 0.4 copy-done.5
  83.3 0.6 convert_reduce_fusion
  84.0 0.5 copy.31
  85.3 0.5 copy.34
  85.8 1.1 copy.26
  86.9 0.6 multiply_bitcast_fusion.2
  87.6 0.8 copy.25
  88.4 26.7 %fusion.25 = f32[1,192,2,256]{1,0,2,3:T(1,128)S(1)} fusion(bf16[1,192,495,1]{1,0,3,2:T(2,128)(2,1)S(1)} %copy.25, bf16[192,2,1,240]{0,2,1,3:T(2,128)(2,1)S(1)} %copy.31), kind=kOutput, calls=%fused_computation.44 | convolution fusion | flops 47185920 | bytes 767616 | tf_op jit(solution)/shard_map/convolution.1
  115.1 0.6 copy.32
  115.9 16.5 %reduce_window.7 = f32[192,256]{0,1:T(8,128)S(1)} reduce-window(f32[192,495]{0,1:T(8,128)S(1)} %copy.28, f32[]{:T(128)} %constant.16.clone.1), window={size=1x240}, to_apply=%region_3.4 | reduce-window | flops 11747328 | bytes 576772 | tf_op jit(solution)/shard_map/reduce_window | solution.py:39
  132.6 26.7 %fusion.26 = f32[1,192,2,256]{1,0,2,3:T(1,128)S(1)} fusion(bf16[1,192,495,1]{1,0,3,2:T(2,128)(2,1)S(1)} %copy.25, bf16[192,2,1,240]{0,2,1,3:T(2,128)(2,1)S(1)} %copy.34), kind=kOutput, calls=%fused_computation.45 | convolution fusion | flops 47185920 | bytes 767616 | tf_op jit(solution)/shard_map/convolution.2
  159.3 0.5 copy.35
  159.8 0.3 fusion.9
  160.1 0.3 fusion.8
  160.5 26.7 %fusion.24 = f32[1,192,2,256]{1,0,2,3:T(1,128)S(1)} fusion(bf16[1,192,495,1]{1,0,3,2:T(2,128)(2,1)S(1)} %copy.25, bf16[192,2,1,240]{0,2,1,3:T(2,128)(2,1)S(1)} %copy-done), kind=kOutput, calls=%fused_computation.43 | convolution fusion | flops 47185920 | bytes 767616 | tf_op jit(solution)/shard_map/convolution
  187.1 0.5 copy.27
  187.6 0.3 fusion.10
  187.9 0.6 pad_maximum_fusion
  (25 shorter events, 0.7 us)
Async XLA Ops:
  0.0 87.5 %collective-permute-start = (bf16[192,239]{1,0:T(8,128)(2,1)}, bf16[192,239]{1,0:T(8,128)(2,1)S(1)}, u32[]{:S(2)}, u32[]{:S(2)}) collective-permute-start(bf16[192,239]{1,0:T(8,128)(2,1)} %bitcast.77), channel_id=1, source_target_pairs={{1,0},{2,1},{3,2},{4,3},{5,4},{6,5},{7,6},{8,7},{9,8},{10,9},{11,1... | collective-permute-start | bytes 275336 | tf_op jit(solution)/shard_map/ppermute | solution.py:10
  82.6 0.7 copy-start.5
  83.3 4.3 %copy-start.1 = (bf16[192,256]{1,0:T(8,128)(2,1)S(1)}, bf16[192,256]{1,0:T(8,128)(2,1)}, u32[]{:S(2)}) copy-start(bf16[192,256]{1,0:T(8,128)(2,1)} %param.5) | copy-start | bytes 294916
  132.6 27.2 %copy-start.4 = (f32[2,192,1]{1,0,2:T(2,128)S(1)}, f32[2,192,1]{1,0,2:T(2,128)}, u32[]{:S(2)}) copy-start(f32[2,192,1]{1,0,2:T(2,128)} %get-tuple-element.10) | copy-start | bytes 4612
  132.6 27.5 %copy-start.3 = (f32[2,192,1]{1,0,2:T(2,128)S(1)}, f32[2,192,1]{1,0,2:T(2,128)}, u32[]{:S(2)}) copy-start(f32[2,192,1]{1,0,2:T(2,128)} %get-tuple-element.9) | copy-start | bytes 4612
  159.3 1.1 copy-start
  160.4 27.2 %copy-start.2 = (f32[2,192,1]{1,0,2:T(2,128)S(1)}, f32[2,192,1]{1,0,2:T(2,128)}, u32[]{:S(2)}) copy-start(f32[2,192,1]{1,0,2:T(2,128)} %get-tuple-element.8) | copy-start | bytes 4612
where the time goes:
time: 189 us
  matrix products  83.5 us (44%)
  blocking collectives  77.2 us (41%)
  other arithmetic  19.4 us (10%)
  local copies, waits for them, and re-layouts  6.15 us (3%)
    another operation x3, matrix products  80 us
    psum x1, blocking collectives, shards(): gathered = lax.psum(contrib, 'tm').astype(jnp.bfloat16)  77.2 us
    another operation x1, other arithmetic, shards(): lax.reduce_window(sq, jnp.array(0.0, sq.dtype), lax.add, (1, taps), (1, 1...  16.5 us
  transfers between devices with their start and end apart: 1, of which 0 were waited for; matrix products, arithmetic and copies ran while one was open for 4% of the time, Pallas kernels for 0%

commit v1 on v0

v1 whole, which is shorter than its diff:
```python
import functools

import jax
import jax.numpy as jnp
from jax import lax
from jax.experimental import pallas as pl
from jax.experimental.pallas import tpu as pltpu
from jax.sharding import PartitionSpec as P

MESH = pl.DeviceIdType.MESH
LANES = 128


def up(value, unit):
    return -(-value // unit) * unit


def kernel(
    n, steps, kcount, taps,
    plan_ref, ids_ref, mask_s, mask_v, rec_ref, bank_ref, out_ref,
    wide, rwide, tsend, rsend, trecv, rrecv, xs, frames, inv, tmpl, wts, acc, osend, orecv,
    ts_sem, tr_sem, rs_sem, rr_sem, os_sem, or_sem,
):
    me = lax.axis_index("tm")
    templates = steps * kcount
    chans, block = rec_ref.shape
    own = chans // n
    halves = block // LANES
    width = frames.shape[2] // LANES

    barrier = pltpu.get_barrier_semaphore()

    @pl.loop(1, n)
    def _(o):
        pl.semaphore_signal(barrier, inc=1, device_id={"tm": lax.rem(me + o, n)}, device_id_type=MESH)

    rec_f = rec_ref[...].astype(jnp.float32)
    for v in range(halves):
        rwide[v] = rec_f[:, v * LANES : (v + 1) * LANES]
    pad = 2 * LANES - taps
    for s in range(steps):
        for k in range(kcount):
            row = (s * kcount + k) * chans
            pick = bank_ref[ids_ref[s, k]].astype(jnp.float32)
            pick = jnp.concatenate([pick, jnp.zeros((chans, pad), jnp.float32)], axis=1)
            for v in range(2):
                wide[v, row : row + chans, :] = pick[:, v * LANES : (v + 1) * LANES]

    @pl.loop(0, n)
    def _(d):
        for v in range(halves):
            rsend[d, :, v * LANES : (v + 1) * LANES] = rwide[v, pl.ds(d, own, stride=n), :].astype(jnp.bfloat16)
        for v in range(2):
            tsend[d, :, v * LANES : (v + 1) * LANES] = wide[v, pl.ds(d, templates * own, stride=n), :].astype(jnp.bfloat16)

    rrecv[me] = rsend[me]
    trecv[me] = tsend[me]

    def hop(send, recv, send_sem, recv_sem, o):
        to = lax.rem(me + o, n)
        return pltpu.make_async_remote_copy(
            src_ref=send.at[to],
            dst_ref=recv.at[me],
            send_sem=send_sem.at[o],
            recv_sem=recv_sem.at[o],
            device_id={"tm": to},
            device_id_type=MESH,
        )

    pl.semaphore_wait(barrier, n - 1)

    @pl.loop(1, n)
    def _(o):
        hop(rsend, rrecv, rs_sem, rr_sem, o).start()

    @pl.loop(1, n)
    def _(o):
        hop(tsend, trecv, ts_sem, tr_sem, o).start()

    @pl.loop(1, n)
    def _(o):
        hop(rsend, rrecv, rs_sem, rr_sem, o).wait()

    for v in range(halves):
        for a in range(n):
            xs[v, a * own : (a + 1) * own, :] = rrecv[a, :, v * LANES : (v + 1) * LANES].astype(jnp.float32)
        xs[v, n * own :, :] = jnp.zeros((xs.shape[1] - n * own, LANES), jnp.float32)
    shift = lax.broadcasted_iota(jnp.int32, (LANES, width * LANES), 1) - lax.broadcasted_iota(
        jnp.int32, (LANES, width * LANES), 0
    )
    band = jnp.where((shift >= 0) & (shift < taps), 1.0, 0.0).astype(jnp.bfloat16)
    live = jnp.sum(mask_v[...].astype(jnp.float32), axis=1, keepdims=True)
    scale = jnp.sqrt(taps / (1.0 + live))

    @pl.loop(0, own)
    def _(i):
        tiles = [
            xs[q % halves, pl.ds(i + (q // halves) * own, n, stride=own), :] for q in range(halves + width - 1)
        ]
        x = jnp.concatenate(
            [jnp.concatenate(tiles[h : h + width], axis=1) for h in range(halves)], axis=0
        )
        frames[i] = x.astype(jnp.bfloat16)
        sq = x * x
        high = sq.astype(jnp.bfloat16)
        low = (sq - high.astype(jnp.float32)).astype(jnp.bfloat16)
        dims = (((1,), (1,)), ((), ()))
        energy = lax.dot_general(high, band, dims, preferred_element_type=jnp.float32)
        energy += lax.dot_general(low, band, dims, preferred_element_type=jnp.float32)
        factor = scale * mask_s[i * n + me].astype(jnp.float32)
        inv[i] = factor / jnp.sqrt(energy + 1e-06)

    @pl.loop(1, n)
    def _(o):
        hop(tsend, trecv, ts_sem, tr_sem, o).wait()

    rows = kcount * own
    for s in range(steps):
        got = trecv[plan_ref[s]].astype(jnp.float32)[s * rows : (s + 1) * rows]
        tmpl[s * rows : (s + 1) * rows, : 2 * LANES] = got
        energy = jnp.sum(got * got, axis=1, keepdims=True)
        wts[s * rows : (s + 1) * rows, :] = jnp.broadcast_to(1.0 / jnp.sqrt(energy + 1e-06), (rows, LANES))
    if width > 2:
        tmpl[:, 2 * LANES :] = jnp.zeros((templates * own, (width - 2) * LANES), jnp.float32)
    acc[...] = jnp.zeros_like(acc)

    @pl.loop(0, own)
    def _(i):
        x = frames[i]
        norm = inv[i]
        for k in range(templates):
            row = k * own + i
            base = jnp.broadcast_to(tmpl[pl.ds(row, 1), :], (LANES, width * LANES))
            toeplitz = pltpu.roll(base, 0, 1, stride=1, stride_axis=0).astype(jnp.bfloat16)
            raw = lax.dot_general(x, toeplitz, (((1,), (1,)), ((), ())), preferred_element_type=jnp.float32)
            part = raw * norm * wts[pl.ds(row, 1), :]
            for h in range(halves):
                at = (h * templates + k) * n
                acc[at : at + n, :] += part[h * n : (h + 1) * n]

    @pl.loop(0, n)
    def _(d):
        osend[d] = acc[pl.ds(d, halves * templates, stride=n), :]

    @pl.loop(1, n)
    def _(o):
        hop(osend, orecv, os_sem, or_sem, o).start()

    total = osend[me]
    orecv[me] = total

    @pl.loop(1, n)
    def _(o):
        hop(osend, orecv, os_sem, or_sem, o).wait()

    final = jnp.sum(orecv[...], axis=0)
    for h in range(halves):
        for s in range(steps):
            at = h * templates + s * kcount
            out_ref[s, :, h * LANES : (h + 1) * LANES] = final[at : at + kcount]


def shards(records, bank, plan, template_ids, channel_mask):
    n = lax.axis_size("tm")
    steps, kcount = template_ids.shape
    chans, block = records.shape
    taps = bank.shape[2]
    own = chans // n
    templates = steps * kcount
    halves = block // LANES
    width = up(LANES + taps - 1, LANES) // LANES
    vmem = pl.BlockSpec(memory_space=pltpu.VMEM)
    smem = pl.BlockSpec(memory_space=pltpu.SMEM)
    f32, bf16 = jnp.float32, jnp.bfloat16
    dma = pltpu.SemaphoreType.DMA((n,))
    extra = -(-(halves + width - 2) // halves)
    return pl.pallas_call(
        functools.partial(kernel, n, steps, kcount, taps),
        out_shape=jax.ShapeDtypeStruct((steps, kcount, block), f32),
        in_specs=[smem, smem, smem, vmem, vmem, vmem],
        out_specs=vmem,
        scratch_shapes=[
            pltpu.VMEM((2, templates * chans, LANES), f32),
            pltpu.VMEM((halves, chans, LANES), f32),
            pltpu.VMEM((n, templates * own, 2 * LANES), bf16),
            pltpu.VMEM((n, own, block), bf16),
            pltpu.VMEM((n, templates * own, 2 * LANES), bf16),
            pltpu.VMEM((n, own, block), bf16),
            pltpu.VMEM((halves, (n + extra) * own, LANES), f32),
            pltpu.VMEM((own, halves * n, width * LANES), bf16),
            pltpu.VMEM((own, halves * n, LANES), f32),
            pltpu.VMEM((templates * own, width * LANES), f32),
            pltpu.VMEM((templates * own, LANES), f32),
            pltpu.VMEM((halves * templates * n, LANES), f32),
            pltpu.VMEM((n, halves * templates, LANES), f32),
            pltpu.VMEM((n, halves * templates, LANES), f32),
            dma, dma, dma, dma, dma, dma,
        ],
        compiler_params=pltpu.CompilerParams(
            collective_id=0, has_side_effects=True, vmem_limit_bytes=60 * 1024 * 1024
        ),
        name="detect",
    )(plan, template_ids, channel_mask, channel_mask.reshape(1, -1), records, bank)


def solution(mesh):
    placed = (
        P("groups", "tm"),
        P("tm", "groups", None),
        P("groups"),
        P("groups", None),
        P("groups"),
    )
    return jax.shard_map(
        shards, mesh=mesh, in_specs=placed, out_specs=P("groups", None, "tm"), check_vma=False
    )
```

time: 189 us -> 38.6 us (0.20)
  matrix products: 83.5 us -> 0 us
  blocking collectives: 77.2 us -> 0 us
  Pallas kernels: 0 us -> 35.8 us
  other arithmetic: 19.4 us -> 0 us
  local copies, waits for them, and re-layouts: 6.15 us -> 2.62 us
    another operation x3 -> x0, matrix products: 80 us -> none
    psum x1 -> x0, blocking collectives: 77.2 us -> none  [shards(): gathered = lax.psum(contrib, 'tm').astype(jnp.bfloat16)]
    pallas_call x0 -> x1, Pallas kernels: none -> 35.8 us  [shards(): pl.pallas_call(functools.partial(kernel, n, steps, kcount, taps), out_sha...]
    another operation x5 -> x0, other arithmetic: 17.1 us -> none  [the longest x1 16.5 us: shards(): lax.reduce_window(sq, jnp.array(0.0, sq.dtype), lax.add, (1, taps), (1, 1...]
    another operation x7 -> x0, local copies, waits for them, and re-layouts: 3.49 us -> none
    dot_general x4 -> x0, matrix products: 3.47 us -> none  [the longest x1 2.53 us: shards(): jnp.einsum('skb,bcl->skcl', onehot, bank, preferred_element_type=jnp.floa...]
    unnamed x14 -> x2, local copies, waits for them, and re-layouts: 0.43 us -> 2.62 us
  transfers between devices with their start and end apart: 1 -> 0, of which waited for: 0 -> 0; matrix products, arithmetic and copies ran while one was open for 4% -> 0% of each run, Pallas kernels for 0% -> 0%
where the time goes in v1:
time: 38.6 us; the launch traced here: 38.4 us
  Pallas kernels  35.8 us (93%)
  local copies, waits for them, and re-layouts  2.62 us (7%)
    pallas_call x1, Pallas kernels, shards(): pl.pallas_call(functools.partial(kernel, n, steps, kcount, taps), out_sha...  35.8 us
    unnamed x2, local copies, waits for them, and re-layouts  2.62 us

profile of v1, /device:TPU:0, one launch (start us, length us, event | category | flops | bytes accessed | tf_op | source)
XLA Modules:
  0.0 38.4 jit_solution(5302224805743965414)
XLA Ops:
  0.0 1.3 %copy.6.ids_ref = s32[3,2]{1,0:T(4,128)} copy(s32[3,2]{0,1:T(2,128)} %param.8) | data formatting | bytes 48 | tf_op args[3]
  1.3 35.8 %detect.1 = f32[3,2,256]{2,1,0:T(2,128)} custom-call(s32[3]{0:T(128)} %plan_ref.1, s32[3,2]{1,0:T(4,128)} %copy.6.ids_ref, s32[192]{0:T(256)} %mask_s.1, s32[1,192]{1,0:T(1,128)} %bitcast.1, bf16[192,256]{1,0:T(8,128)(2,1)} %rec_ref.1, bf16[16,192,240]{2,1,0:T(8,128)(2,1)} %bank_ref.1), custom_call_target="tpu_custom_call" | custom-call | tf_op jit(solution)/shard_map/detect/pallas_call | solution.py:177
  37.2 1.3 %copy.8 = f32[3,2,256]{2,1,0:T(2,128)} copy(f32[3,2,256]{2,1,0:T(2,128)} %detect.1) | data formatting | bytes 12288

commit v2 on v1

v2 whole, which is shorter than its diff:
```python
import functools

import jax
import jax.numpy as jnp
from jax import lax
from jax.experimental import pallas as pl
from jax.experimental.pallas import tpu as pltpu
from jax.sharding import PartitionSpec as P

MESH = pl.DeviceIdType.MESH
LANES = 128


def up(value, unit):
    return -(-value // unit) * unit


def kernel(
    n, steps, kcount, taps, unroll,
    plan_ref, ids_ref, mask_s, mask_v, rec_ref, bank_ref, out_ref,
    wide, rwide, tsend, tpart, tcomb, rsend, trecv, rrecv, xs, frames, inv, tmpl, wts, acc, osend, orecv,
    cs_sem, cr_sem, ts_sem, tr_sem, rs_sem, rr_sem, os_sem, or_sem,
):
    me = lax.axis_index("tm")
    chip, core = me // 2, me % 2
    chips = n // 2
    partner = me + 1 - 2 * core
    chans, block = rec_ref.shape
    own = chans // n
    rows = kcount * own
    halves = block // LANES
    width = frames.shape[2] // LANES
    dims = (((1,), (1,)), ((), ()))

    barrier = pltpu.get_barrier_semaphore()

    @pl.loop(1, n)
    def _(o):
        pl.semaphore_signal(barrier, inc=1, device_id={"tm": lax.rem(me + o, n)}, device_id_type=MESH)

    rec_f = rec_ref[...].astype(jnp.float32)
    for v in range(halves):
        rwide[v] = rec_f[:, v * LANES : (v + 1) * LANES]
    pad = 2 * LANES - taps
    for s in range(steps):
        for k in range(kcount):
            pick = bank_ref[ids_ref[s, k]].astype(jnp.float32)
            pick = jnp.concatenate([pick, jnp.zeros((chans, pad), jnp.float32)], axis=1)
            for v in range(2):
                wide[s, v, k * chans : (k + 1) * chans, :] = pick[:, v * LANES : (v + 1) * LANES]

    @pl.loop(0, n)
    def _(d):
        for v in range(halves):
            rsend[d, :, v * LANES : (v + 1) * LANES] = rwide[v, pl.ds(d, own, stride=n), :].astype(jnp.bfloat16)
        for s in range(steps):
            for v in range(2):
                tsend[s, d % 2, d // 2, :, v * LANES : (v + 1) * LANES] = wide[
                    s, v, pl.ds(d, rows, stride=n), :
                ].astype(jnp.bfloat16)

    rrecv[me] = rsend[me]

    def hop(send, recv, send_sem, recv_sem, o):
        to = lax.rem(me + o, n)
        return pltpu.make_async_remote_copy(
            src_ref=send.at[to], dst_ref=recv.at[me], send_sem=send_sem.at[o], recv_sem=recv_sem.at[o],
            device_id={"tm": to}, device_id_type=MESH,
        )

    def across(s):
        return pltpu.make_async_remote_copy(
            src_ref=tsend.at[s, 1 - core], dst_ref=tpart.at[s], send_sem=cs_sem.at[s], recv_sem=cr_sem.at[s],
            device_id={"tm": partner}, device_id_type=MESH,
        )

    def spread(s, o):
        to = lax.rem(chip + o, chips)
        return pltpu.make_async_remote_copy(
            src_ref=tcomb.at[s, to], dst_ref=trecv[s].at[chip], send_sem=ts_sem.at[s, o], recv_sem=tr_sem.at[s, o],
            device_id={"tm": 2 * to + core}, device_id_type=MESH,
        )

    pl.semaphore_wait(barrier, n - 1)
    for s in range(steps):
        across(s).start()

    @pl.loop(1, n)
    def _(o):
        hop(rsend, rrecv, rs_sem, rr_sem, o).start()

    for s in range(steps):
        across(s).wait_recv()
        theirs = plan_ref[s] == partner
        mix = jnp.where(theirs, tpart[s].astype(jnp.float32), tsend[s, core].astype(jnp.float32))
        tcomb[s] = mix.astype(jnp.bfloat16)
        trecv[s][chip] = tcomb[s, chip]

        @pl.loop(1, chips)
        def _(o):
            spread(s, o).start()

    @pl.loop(1, n)
    def _(o):
        hop(rsend, rrecv, rs_sem, rr_sem, o).wait_recv()

    for v in range(halves):
        for a in range(n):
            xs[v, a * own : (a + 1) * own, :] = rrecv[a, :, v * LANES : (v + 1) * LANES].astype(jnp.float32)
        xs[v, n * own :, :] = jnp.zeros((xs.shape[1] - n * own, LANES), jnp.float32)
    shift = lax.broadcasted_iota(jnp.int32, (LANES, width * LANES), 1) - lax.broadcasted_iota(
        jnp.int32, (LANES, width * LANES), 0
    )
    band = jnp.where((shift >= 0) & (shift < taps), 1.0, 0.0).astype(jnp.bfloat16)
    live = jnp.sum(mask_v[...].astype(jnp.float32), axis=1, keepdims=True)
    scale = jnp.sqrt(taps / (1.0 + live))

    def frame(i, carry):
        tiles = [
            xs[q % halves, pl.ds(i + (q // halves) * own, n, stride=own), :] for q in range(halves + width - 1)
        ]
        x = jnp.concatenate(
            [jnp.concatenate(tiles[h : h + width], axis=1) for h in range(halves)], axis=0
        )
        frames[i] = x.astype(jnp.bfloat16)
        sq = x * x
        high = sq.astype(jnp.bfloat16)
        low = (sq - high.astype(jnp.float32)).astype(jnp.bfloat16)
        energy = lax.dot_general(
            jnp.concatenate([high, low], axis=0), band, dims, preferred_element_type=jnp.float32
        )
        energy = energy[: halves * n] + energy[halves * n :]
        factor = scale * mask_s[i * n + me].astype(jnp.float32)
        inv[i] = factor / jnp.sqrt(energy + 1e-06)
        return carry

    lax.fori_loop(0, own, frame, 0, unroll=unroll)
    if width > 2:
        tmpl[:, 2 * LANES :] = jnp.zeros((rows, (width - 2) * LANES), jnp.float32)

    for s in range(steps):

        @pl.loop(1, chips)
        def _(o):
            spread(s, o).wait_recv()

        got = trecv[s][lax.div(plan_ref[s], 2)].astype(jnp.float32)
        tmpl[:, : 2 * LANES] = got
        energy = jnp.sum(got * got, axis=1, keepdims=True)
        wts[...] = jnp.broadcast_to(1.0 / jnp.sqrt(energy + 1e-06), (rows, LANES))
        acc[s] = jnp.zeros(acc.shape[1:], jnp.float32)

        def channel(i, carry):
            banks = []
            for k in range(kcount):
                base = jnp.broadcast_to(tmpl[pl.ds(k * own + i, 1), :], (16, width * LANES)).astype(jnp.bfloat16)
                base = jnp.concatenate([base] * (LANES // 16), axis=0)
                banks.append(pltpu.roll(base, 0, 1, stride=1, stride_axis=0))
            raw = lax.dot_general(
                frames[i], jnp.concatenate(banks, axis=0), dims, preferred_element_type=jnp.float32
            )
            norm = inv[i]
            for k in range(kcount):
                part = raw[:, k * LANES : (k + 1) * LANES] * norm * wts[pl.ds(k * own + i, 1), :]
                for h in range(halves):
                    at = (h * kcount + k) * n
                    acc[s, at : at + n, :] += part[h * n : (h + 1) * n]
            return carry

        lax.fori_loop(0, own, channel, 0, unroll=unroll)

        for d in range(n):
            osend[s, d] = acc[s, pl.ds(d, halves * kcount, stride=n), :]
        orecv[s, me] = osend[s, me]

        @pl.loop(1, n)
        def _(o):
            hop(osend.at[s], orecv.at[s], os_sem.at[s], or_sem.at[s], o).start()

    for s in range(steps):

        @pl.loop(1, n)
        def _(o):
            hop(osend.at[s], orecv.at[s], os_sem.at[s], or_sem.at[s], o).wait_recv()

        final = jnp.sum(orecv[s], axis=0)
        for h in range(halves):
            out_ref[s, :, h * LANES : (h + 1) * LANES] = final[h * kcount : (h + 1) * kcount]

    for s in range(steps):
        across(s).wait_send()

        @pl.loop(1, chips)
        def _(o):
            spread(s, o).wait_send()

        @pl.loop(1, n)
        def _(o):
            hop(osend.at[s], orecv.at[s], os_sem.at[s], or_sem.at[s], o).wait_send()

    @pl.loop(1, n)
    def _(o):
        hop(rsend, rrecv, rs_sem, rr_sem, o).wait_send()


def shards(records, bank, plan, template_ids, channel_mask):
    n = lax.axis_size("tm")
    steps, kcount = template_ids.shape
    chans, block = records.shape
    taps = bank.shape[2]
    own = chans // n
    rows = kcount * own
    halves = block // LANES
    width = up(LANES + taps - 1, LANES) // LANES
    vmem = pl.BlockSpec(memory_space=pltpu.VMEM)
    smem = pl.BlockSpec(memory_space=pltpu.SMEM)
    f32, bf16 = jnp.float32, jnp.bfloat16
    dma = pltpu.SemaphoreType.DMA
    extra = -(-(halves + width - 2) // halves)
    return pl.pallas_call(
        functools.partial(kernel, n, steps, kcount, taps, min(own, 4)),
        out_shape=jax.ShapeDtypeStruct((steps, kcount, block), f32),
        in_specs=[smem, smem, smem, vmem, vmem, vmem],
        out_specs=vmem,
        scratch_shapes=[
            pltpu.VMEM((steps, 2, kcount * chans, LANES), f32),
            pltpu.VMEM((halves, chans, LANES), f32),
            pltpu.VMEM((steps, 2, n // 2, rows, 2 * LANES), bf16),
            pltpu.VMEM((steps, n // 2, rows, 2 * LANES), bf16),
            pltpu.VMEM((steps, n // 2, rows, 2 * LANES), bf16),
            pltpu.VMEM((n, own, block), bf16),
            [pltpu.VMEM((n // 2, rows, 2 * LANES), bf16)] * steps,
            pltpu.VMEM((n, own, block), bf16),
            pltpu.VMEM((halves, (n + extra) * own, LANES), f32),
            pltpu.VMEM((own, halves * n, width * LANES), bf16),
            pltpu.VMEM((own, halves * n, LANES), f32),
            pltpu.VMEM((rows, width * LANES), f32),
            pltpu.VMEM((rows, LANES), f32),
            pltpu.VMEM((steps, halves * kcount * n, LANES), f32),
            pltpu.VMEM((steps, n, halves * kcount, LANES), f32),
            pltpu.VMEM((steps, n, halves * kcount, LANES), f32),
            dma((steps,)), dma((steps,)), dma((steps, n // 2)), dma((steps, n // 2)),
            dma((n,)), dma((n,)), dma((steps, n)), dma((steps, n)),
        ],
        compiler_params=pltpu.CompilerParams(
            collective_id=0, has_side_effects=True, vmem_limit_bytes=60 * 1024 * 1024
        ),
        name="detect",
    )(plan, template_ids, channel_mask, channel_mask.reshape(1, -1), records, bank)


def solution(mesh):
    placed = (
        P("groups", "tm"),
        P("tm", "groups", None),
        P("groups"),
        P("groups", None),
        P("groups"),
    )
    return jax.shard_map(
        shards, mesh=mesh, in_specs=placed, out_specs=P("groups", None, "tm"), check_vma=False
    )
```

time: 38.6 us -> 31.1 us (0.81)
  Pallas kernels: 35.8 us -> 28.3 us
    pallas_call x1, Pallas kernels: 35.8 us -> 28.3 us  [shards(): pl.pallas_call(functools.partial(kernel, n, steps, kcount, taps, min(own,...]
where the time goes in v2:
time: 31.1 us; the launch traced here: 30.9 us
  Pallas kernels  28.3 us (91%)
  local copies, waits for them, and re-layouts  2.62 us (8%)
    pallas_call x1, Pallas kernels, shards(): pl.pallas_call(functools.partial(kernel, n, steps, kcount, taps, min(own,...  28.3 us
    unnamed x2, local copies, waits for them, and re-layouts  2.62 us

profile of v2, /device:TPU:0, one launch (start us, length us, event | category | flops | bytes accessed | tf_op | source)
XLA Modules:
  0.0 30.9 jit_solution(1258863832710175688)
XLA Ops:
  0.0 1.3 %copy.6.ids_ref = s32[3,2]{1,0:T(4,128)} copy(s32[3,2]{0,1:T(2,128)} %param.8) | data formatting | bytes 48 | tf_op args[3]
  1.3 28.3 %detect.1 = f32[3,2,256]{2,1,0:T(2,128)} custom-call(s32[3]{0:T(128)} %plan_ref.1, s32[3,2]{1,0:T(4,128)} %copy.6.ids_ref, s32[192]{0:T(256)} %mask_s.1, s32[1,192]{1,0:T(1,128)} %bitcast.1, bf16[192,256]{1,0:T(8,128)(2,1)} %rec_ref.1, bf16[16,192,240]{2,1,0:T(8,128)(2,1)} %bank_ref.1), custom_call_target="tpu_custom_call" | custom-call | tf_op jit(solution)/shard_map/detect/pallas_call | solution.py:220
  29.6 1.3 %copy.8 = f32[3,2,256]{2,1,0:T(2,128)} copy(f32[3,2,256]{2,1,0:T(2,128)} %detect.1) | data formatting | bytes 12288

commit v3 on v2

--- a/solution.py
+++ b/solution.py
@@ -18,8 +18,8 @@
 def kernel(
     n, steps, kcount, taps, unroll,
     plan_ref, ids_ref, mask_s, mask_v, rec_ref, bank_ref, out_ref,
-    wide, rwide, tsend, tpart, tcomb, rsend, trecv, rrecv, xs, frames, inv, tmpl, wts, acc, osend, orecv,
-    cs_sem, cr_sem, ts_sem, tr_sem, rs_sem, rr_sem, os_sem, or_sem,
+    wide, rwide, tsend, tpart, tcomb, rsend, trecv, rrecv, xs, frames, inv, tmpl, wts, acc, osend, orecv, bank_v,
+    bank_sem, cs_sem, cr_sem, ts_sem, tr_sem, rs_sem, rr_sem, os_sem, or_sem,
 ):
     me = lax.axis_index("tm")
     chip, core = me // 2, me % 2
@@ -38,13 +38,17 @@
     def _(o):
         pl.semaphore_signal(barrier, inc=1, device_id={"tm": lax.rem(me + o, n)}, device_id_type=MESH)
 
+    fetch = pltpu.make_async_copy(bank_ref, bank_v, bank_sem)
+    fetch.start()
+
     rec_f = rec_ref[...].astype(jnp.float32)
     for v in range(halves):
         rwide[v] = rec_f[:, v * LANES : (v + 1) * LANES]
     pad = 2 * LANES - taps
+    fetch.wait()
     for s in range(steps):
         for k in range(kcount):
-            pick = bank_ref[ids_ref[s, k]].astype(jnp.float32)
+            pick = bank_v[ids_ref[k, s]].astype(jnp.float32)
             pick = jnp.concatenate([pick, jnp.zeros((chans, pad), jnp.float32)], axis=1)
             for v in range(2):
                 wide[s, v, k * chans : (k + 1) * chans, :] = pick[:, v * LANES : (v + 1) * LANES]
@@ -98,7 +102,7 @@
 
         @pl.loop(1, chips)
         def _(o):
-            spread(s, o).start()
+            spread(s, lax.rem(o + chips // 2 - 1, chips - 1) + 1).start()
 
     @pl.loop(1, n)
     def _(o):
@@ -218,9 +222,9 @@
     dma = pltpu.SemaphoreType.DMA
     extra = -(-(halves + width - 2) // halves)
     return pl.pallas_call(
-        functools.partial(kernel, n, steps, kcount, taps, min(own, 4)),
+        functools.partial(kernel, n, steps, kcount, taps, own),
         out_shape=jax.ShapeDtypeStruct((steps, kcount, block), f32),
-        in_specs=[smem, smem, smem, vmem, vmem, vmem],
+        in_specs=[smem, smem, smem, vmem, vmem, pl.BlockSpec(memory_space=pl.ANY)],
         out_specs=vmem,
         scratch_shapes=[
             pltpu.VMEM((steps, 2, kcount * chans, LANES), f32),
@@ -239,14 +243,15 @@
             pltpu.VMEM((steps, halves * kcount * n, LANES), f32),
             pltpu.VMEM((steps, n, halves * kcount, LANES), f32),
             pltpu.VMEM((steps, n, halves * kcount, LANES), f32),
-            dma((steps,)), dma((steps,)), dma((steps, n // 2)), dma((steps, n // 2)),
+            pltpu.VMEM(bank.shape, bf16),
+            dma(()), dma((steps,)), dma((steps,)), dma((steps, n // 2)), dma((steps, n // 2)),
             dma((n,)), dma((n,)), dma((steps, n)), dma((steps, n)),
         ],
         compiler_params=pltpu.CompilerParams(
             collective_id=0, has_side_effects=True, vmem_limit_bytes=60 * 1024 * 1024
         ),
         name="detect",
-    )(plan, template_ids, channel_mask, channel_mask.reshape(1, -1), records, bank)
+    )(plan, template_ids.T, channel_mask, channel_mask.reshape(1, -1), records, bank)
 
 
 def solution(mesh):

time: 31.1 us -> 27.4 us (0.88)
  Pallas kernels: 28.3 us -> 25.9 us
  local copies, waits for them, and re-layouts: 2.62 us -> 1.29 us
    pallas_call x1, Pallas kernels: 28.3 us -> 25.9 us  [shards(): pl.pallas_call(functools.partial(kernel, n, steps, kcount, taps, own), ou...]
    unnamed x2 -> x1, local copies, waits for them, and re-layouts: 2.62 us -> 1.29 us
where the time goes in v3:
time: 27.4 us; the launch traced here: 27.2 us
  Pallas kernels  25.9 us (95%)
  local copies, waits for them, and re-layouts  1.29 us (5%)
    pallas_call x1, Pallas kernels, shards(): pl.pallas_call(functools.partial(kernel, n, steps, kcount, taps, own), ou...  25.9 us
    unnamed x1, local copies, waits for them, and re-layouts  1.29 us

profile of v3, /device:TPU:0, one launch (start us, length us, event | category | flops | bytes accessed | tf_op | source)
XLA Modules:
  0.0 27.2 jit_solution(14230827014548306768)
XLA Ops:
  0.0 25.9 %detect.1 = f32[3,2,256]{2,1,0:T(2,128)} custom-call(s32[3]{0:T(128)} %plan_ref.1, s32[2,3]{1,0:T(2,128)} %bitcast.3, s32[192]{0:T(256)} %mask_s.1, s32[1,192]{1,0:T(1,128)} %bitcast.2, bf16[192,256]{1,0:T(8,128)(2,1)} %rec_ref.1, bf16[16,192,240]{2,1,0:T(8,128)(2,1)} %bank_ref.1), custom_call_target="tpu_custom_call" | custom-call | tf_op jit(solution)/shard_map/detect/pallas_call | solution.py:224
  25.9 1.3 %copy.7 = f32[3,2,256]{2,1,0:T(2,128)} copy(f32[3,2,256]{2,1,0:T(2,128)} %detect.1) | data formatting | bytes 12288
